TPU v7x, 32 devices: a whole 2x2x4 slice. The times are simulated.
32 devices in a mesh: vocab: 8 (over z, y), feat: 4 (over x, core).
Axes of the slice: x: 2, y: 2, z: 4, core: 2. Of those that a mesh axis runs over, the one named last changes fastest.
Arguments:
- hidden: bfloat16 [1024, 4096], P('feat'), may hold values from -64 to 64
- out_head: bfloat16 [32768, 4096], P(('vocab', 'feat')), may hold values from -0.28125 to 0.28125
- out_proj: bfloat16 [32768, 128], P(('vocab', 'feat')), may hold values from -5 to 5
- in_proj: bfloat16 [4096, 128], replicated, may hold values from -0.09375 to 0.09375
- targets: int32 [1024], replicated, may hold values from 0 to 32767
- seq_ids: int32 [1024], replicated, may hold values from 0 to 15, never falling along the last dimension, each value on 1 to 128 neighbouring positions
- grad_store: bfloat16 [16384, 16384], P('vocab', 'feat'), may hold values from -0.01953125 to 0.01953125
Outputs:
- influence: float32 [16384, 16], P(('vocab', 'feat'))
All inputs are finite; a program needn't handle non-finite values.
Results may differ from a plain program's by a relative error of at most 0.003.
Values may be sent and summed in bfloat16 or wider, within the bound.
A program may use at most 128 MiB of HBM per device.

v0:
```python
import jax
import jax.numpy as jnp
from jax import lax
from jax.sharding import PartitionSpec as P

SEQS = 16


def on_device(hidden, out_head, out_proj, in_proj, targets, seq_ids, grad_store):
    vocab_local = out_head.shape[0]
    tok_piece = lax.all_gather(hidden, "feat", axis=0, tiled=True)
    logits = lax.dot_general(
        tok_piece, out_head, (((1,), (1,)), ((), ())), preferred_element_type=jnp.float32
    )
    projected = jnp.dot(tok_piece, in_proj, preferred_element_type=jnp.float32)
    joined = jnp.concatenate([logits, projected], axis=1)
    logits = joined[:, :vocab_local]
    in_side = joined[:, vocab_local:]
    local_max = jnp.max(logits, axis=1)
    global_max = lax.pmax(local_max, ("vocab", "feat"))
    expval = jnp.exp(logits - global_max[:, None])
    global_sum = lax.psum(jnp.sum(expval, axis=1), ("vocab", "feat"))
    offset = lax.axis_index(("vocab", "feat")) * vocab_local
    columns = offset + lax.iota(jnp.int32, vocab_local)
    onehot = (targets[:, None] == columns[None, :]).astype(jnp.float32)
    residual = (expval / global_sum[:, None] - onehot).astype(jnp.bfloat16)
    partial_out = jnp.dot(residual, out_proj, preferred_element_type=jnp.float32)
    proj_rank = out_proj.shape[1]
    col_share = proj_rank // lax.axis_size("feat")
    feat_cols = lax.psum_scatter(partial_out, "feat", scatter_dimension=1, tiled=True)
    out_part = lax.psum(feat_cols, "vocab")
    tok_total = out_part.shape[0]
    member = (seq_ids[:, None] == lax.iota(jnp.int32, SEQS)[None, :]).astype(jnp.float32)
    weighted = (member[:, :, None] * out_part[:, None, :]).reshape(tok_total, SEQS * col_share)
    query_grads = lax.dot_general(
        weighted,
        in_side,
        (((0,), (0,)), ((), ())),
        precision=lax.Precision.HIGHEST,
        preferred_element_type=jnp.float32,
    )
    query_grads = query_grads.reshape(SEQS, col_share * proj_rank).astype(jnp.bfloat16)
    return lax.psum_scatter(
        lax.dot_general(
            grad_store, query_grads, (((1,), (1,)), ((), ())), preferred_element_type=jnp.float32
        ),
        "feat",
        scatter_dimension=0,
        tiled=True,
    )


def solution(mesh):
    in_specs = (
        P("feat", None),
        P(("vocab", "feat"), None),
        P(("vocab", "feat"), None),
        P(),
        P(),
        P(),
        P("vocab", "feat"),
    )
    out_specs = P(("vocab", "feat"), None)
    return jax.shard_map(
        on_device, mesh=mesh, in_specs=in_specs, out_specs=out_specs, check_vma=False
    )
```

profile of v0, /device:TPU:0, one launch (start us, length us, event | category | flops | bytes accessed | tf_op | source)
XLA Modules:
  0.0 307.0 jit_solution(16104171365055655908)
XLA Ops:
  6.5 0.0 copy-start
  6.5 0.0 all-gather.2.cloned.1.call-start
  6.5 0.7 all-gather.2.cloned.1.call-update
  7.3 0.0 reduce-scatter.3.cloned.1.call-start
  7.3 62.6 %all-gather.2.cloned.1.call-done = bf16[1024,4096]{1,0:T(8,128)(2,1)} async-done(((bf16[256,4096]{1,0:T(8,128)(2,1)}), bf16[1024,4096]{1,0:T(8,128)(2,1)}) %all-gather.2.cloned.1.call-update) | async-done | bytes 8388624 | tf_op jit(solution)/shard_map/all_gather | solution.py:11
  69.9 15.0 %fusion.3 = (f32[1024]{0:T(1024)S(1)}, f32[1024,1024]{0,1:T(8,128)}) fusion(bf16[1024,4096]{1,0:T(8,128)(2,1)} %all-gather.2.cloned.1.call-done, bf16[1024,4096]{1,0:T(8,128)(2,1)} %param.8), kind=kOutput, calls=%fused_computation.10 | convolution fusion | flops 8590982144 | bytes 20975616 | tf_op jit(solution)/shard_map/dot_general | solution.py:12
  84.9 0.0 copy-start.2
  84.9 0.0 copy-start.3
  84.9 39.3 %pmax.7 = f32[1024]{0:T(1024)S(1)} all-reduce(f32[1024]{0:T(1024)S(1)} %get-tuple-element.5), channel_id=1, replica_groups=mesh['vocab'=8,'feat'=4] {'vocab','feat'}, use_global_device_ids=true, to_apply=%region_1.0 | all-reduce | flops 1024 | bytes 8192 | tf_op jit(solution)/shard_map/pmax | solution.py:20
  124.2 2.8 fusion
  127.0 41.0 %psum.14 = f32[1024]{0:T(1024)S(1)} all-reduce(f32[1024]{0:T(1024)S(1)} %fusion), channel_id=1, replica_groups=mesh['vocab'=8,'feat'=4] {'vocab','feat'}, use_global_device_ids=true, to_apply=%region_3.0 | all-reduce | flops 1024 | bytes 8192 | tf_op jit(solution)/shard_map/psum | solution.py:22
  168.0 0.0 copy-done.2
  168.0 0.0 copy-done.3
  168.0 0.0 copy-start.1
  168.0 4.3 %fusion.1 = f32[1024,128]{0,1:T(8,128)} fusion(bf16[1024,128]{1,0:T(8,128)(2,1)S(1)} %copy-done.2, f32[1024,1024]{0,1:T(8,128)} %get-tuple-element.6, s32[1024]{0:T(1024)S(1)} %copy-done.3, f32[1024]{0:T(1024)S(1)} %psum.14, f32[1024]{0:T(1024)S(1)} %pmax.7, s32[1024]{0:T(1024)S(1)} %iota_add_fusion), kind=kOutput, calls=%fused_computation.4 | convolution fusion | flops 274726912 | bytes 4997120 | tf_op jit(solution)/shard_map/dot_general | solution.py:27
  172.3 0.0 reduce-scatter.3.cloned.1.call-update
  172.3 0.0 all-reduce.2.cloned.1.call-start
  172.4 0.0 copy-done.1
  172.4 21.5 %reduce-scatter.3.cloned.1.call-done = f32[1024,32]{0,1:T(8,128)} async-done(((f32[1024,128]{0,1:T(8,128)}), f32[1024,32]{0,1:T(8,128)}) %reduce-scatter.3.cloned.1.call-update) | async-done | bytes 131088 | tf_op jit(solution)/shard_map/reduce_scatter | solution.py:30
  193.9 0.0 all-reduce.2.cloned.1.call-update
  193.9 0.2 reduce-scatter.5.cloned.1.call-start
  194.2 0.0 copy-done
  194.2 5.7 %fusion.4 = f32[1024,128]{1,0:T(8,128)S(1)} fusion(bf16[1024,4096]{1,0:T(8,128)(2,1)} %all-gather.2.cloned.1.call-done, bf16[4096,128]{1,0:T(8,128)(2,1)S(1)} %copy-done), kind=kOutput, calls=%fused_computation.11 | convolution fusion | flops 1073741824 | bytes 9961472 | tf_op jit(solution)/shard_map/dot_general | solution.py:15
  199.9 67.8 %all-reduce.2.cloned.1.call-done = f32[1024,32]{0,1:T(8,128)} async-done(((f32[1024,32]{0,1:T(8,128)}), f32[1024,32]{0,1:T(8,128)}) %all-reduce.2.cloned.1.call-update) | async-done | bytes 131088 | tf_op jit(solution)/shard_map/psum | solution.py:31
  267.7 1.1 broadcast_multiply_fusion
  268.8 1.8 convolution_convert_fusion
  270.6 0.1 convert_element_type.23
  270.7 10.8 %convolution_bitcast_fusion = f32[2048,16]{0,1:T(8,128)} fusion(bf16[16,4096]{1,0:T(8,128)(2,1)S(1)} %convert_element_type.23, bf16[2048,4096]{1,0:T(8,128)(2,1)} %param.13), kind=kOutput, calls=%fused_computation.3 | convolution fusion | flops 268435456 | bytes 17039360 | tf_op jit(solution)/shard_map/dot_general | solution.py:44
  281.5 0.0 reduce-scatter.5.cloned.1.call-update
  281.6 18.9 %reduce-scatter.5.cloned.1.call-done = f32[512,16]{0,1:T(8,128)} async-done(((f32[2048,16]{0,1:T(8,128)}), f32[512,16]{0,1:T(8,128)}) %reduce-scatter.5.cloned.1.call-update) | async-done | bytes 32784 | tf_op jit(solution)/shard_map/reduce_scatter | solution.py:43
  (2 shorter events, 0.0 us)
Async XLA Ops:
  6.5 187.6 %copy-start = (bf16[4096,128]{1,0:T(8,128)(2,1)S(1)}, bf16[4096,128]{1,0:T(8,128)(2,1)}, u32[]{:S(2)}) copy-start(bf16[4096,128]{1,0:T(8,128)(2,1)} %param.10) | copy-start | bytes 3145732
  6.5 63.4 %all-gather.2.cloned.1.call-start = ((), (), s32[]{:S(2)}) async-start(), calls=%async_computation.2 | async-start | bytes 10485760 | tf_op jit(solution)/shard_map/all_gather | solution.py:11
  7.3 186.6 %reduce-scatter.3.cloned.1.call-start = ((), (), s32[]{:S(2)}) async-start(), calls=%async_computation.3 | async-start | bytes 655360 | tf_op jit(solution)/shard_map/reduce_scatter | solution.py:30
  84.9 83.1 %copy-start.2 = (bf16[1024,128]{1,0:T(8,128)(2,1)S(1)}, bf16[1024,128]{1,0:T(8,128)(2,1)}, u32[]{:S(2)}) copy-start(bf16[1024,128]{1,0:T(8,128)(2,1)} %param.9) | copy-start | bytes 786436
  84.9 83.1 %copy-start.3 = (s32[1024]{0:T(1024)S(1)}, s32[1024]{0:T(1024)}, u32[]{:S(2)}) copy-start(s32[1024]{0:T(1024)} %param.11) | copy-start | bytes 12292
  168.0 4.4 %copy-start.1 = (s32[1024]{0:T(1024)S(1)}, s32[1024]{0:T(1024)}, u32[]{:S(2)}) copy-start(s32[1024]{0:T(1024)} %param.12) | copy-start | bytes 12292
  172.3 95.3 %all-reduce.2.cloned.1.call-start = ((), (), s32[]{:S(2)}) async-start(), calls=%async_computation.4 | async-start | bytes 262144 | tf_op jit(solution)/shard_map/psum | solution.py:31
  193.9 106.5 %reduce-scatter.5.cloned.1.call-start = ((), (), s32[]{:S(2)}) async-start(), calls=%async_computation.5 | async-start | bytes 163840 | tf_op jit(solution)/shard_map/reduce_scatter | solution.py:43
Sparse Core Ops, SparseCore 0:
  8.9 60.9 all-gather.1
  172.5 21.3 reduce-scatter.2
  197.2 70.3 all-reduce.1
  281.7 18.7 reduce-scatter.4
where the time goes:
time: 307 us
  waiting for transfers between devices  172 us (56%)
  blocking collectives  80.3 us (26%)
  matrix products  37.7 us (12%)
  between operations  13.2 us (4%)
  other arithmetic  3.97 us (1%)
    psum x1, waiting for transfers between devices, on_device(): out_part = lax.psum(feat_cols, 'vocab')  67.8 us
    all_gather x1, waiting for transfers between devices, on_device(): tok_piece = lax.all_gather(hidden, 'feat', axis=0, tiled=True)  62.6 us
    psum x1, blocking collectives, on_device(): global_sum = lax.psum(jnp.sum(expval, axis=1), ('vocab', 'feat'))  41 us
    pmax x1, blocking collectives, on_device(): global_max = lax.pmax(local_max, ('vocab', 'feat'))  39.3 us
    reduce_scatter x1, waiting for transfers between devices, on_device(): lax.psum_scatter(partial_out, 'feat', scatter_dimension=1, tiled=True)  21.5 us
    reduce_scatter x1, waiting for transfers between devices, on_device(): lax.psum_scatter(lax.dot_general(grad_store, query_grads, (((1,), (1,)),...  18.9 us
    dot_general x1, matrix products, on_device(): lax.dot_general(tok_piece, out_head, (((1,), (1,)), ((), ())), preferred_...  15 us
    dot_general x1, matrix products, on_device(): lax.dot_general(grad_store, query_grads, (((1,), (1,)), ((), ())), prefer...  10.8 us
  transfers between devices with their start and end apart: 4, of which 4 were waited for; matrix products, arithmetic and copies ran while one was open for 2% of the time, Pallas kernels for 0%

commit v1 on v0

v1 whole, which is shorter than its diff:
```python
import functools

import jax
import jax.numpy as jnp
from jax import lax
from jax.experimental import pallas as pl
from jax.experimental.pallas import tpu as pltpu
from jax.sharding import PartitionSpec as P

SEQS = 16
SUBS = 4
F32 = jnp.float32
BF16 = jnp.bfloat16
NT = (((1,), (1,)), ((), ()))


def kernel(nv, nf, hid_in, head_in, oproj, iproj_in, targets, seqs, gs_in, out,
           hid, head, iproj, gs, lg, o_t, o_full, ins, sv, so, st, rv, ro, rst, osb, qg, qgm, part, infl,
           load_sem, x_send, y_send, z_send, s_send, recv, s_recv, own_sems,
           sv_send, so_send, st_send, rv_sem, ro_sem, rst_sem, ag_send, ag_recv, in_send, in_recv, loc_sem):
    v = lax.axis_index("vocab")
    f = lax.axis_index("feat")
    me = v * nf + f
    nd = nv * nf
    x, k = f // 2, f % 2
    xn = nf // 2
    sib = f + 1 - 2 * k
    vy = v + 1 - 2 * (v % 2)
    vz = v + 2 - 4 * ((v // 2) % 2)
    tl = hid.shape[1]
    vl = head.shape[0]
    rank = oproj.shape[1]
    rf, tb = sv.shape[1], sv.shape[2]
    bpc = tl // tb
    eo = out.shape[1]
    piece = tl // 4
    sr = piece // SUBS

    loads = [
        pltpu.make_async_copy(hid_in, hid.at[f], load_sem.at[0]),
        pltpu.make_async_copy(head_in, head, load_sem.at[1]),
        pltpu.make_async_copy(iproj_in, iproj, load_sem.at[2]),
        pltpu.make_async_copy(gs_in, gs, load_sem.at[3]),
    ]
    loads[0].start()
    loads[1].start()
    loads[2].start()

    barrier = pltpu.get_barrier_semaphore()

    def greet(p, c):
        d = (me + p) % nd
        pl.semaphore_signal(barrier, inc=1, device_id={"vocab": d // nf, "feat": d % nf},
                            device_id_type=pl.DeviceIdType.MESH)
        return c

    lax.fori_loop(1, nd, greet, 0)
    pl.semaphore_wait(barrier, nd - 1)

    def remote(src, dst, ss, rs, dv, df):
        return pltpu.make_async_remote_copy(
            src_ref=src, dst_ref=dst, send_sem=ss, recv_sem=rs,
            device_id={"vocab": dv, "feat": df}, device_id_type=pl.DeviceIdType.MESH)

    def rows(fi, owner, j):
        return hid.at[fi, pl.ds(pl.multiple_of((owner % 4) * piece + j * sr, sr), sr)]

    pending = []

    def go(copy):
        copy.start()
        pending.append(copy)

    loads[0].wait()
    for r in range(xn - 1):
        fo = 2 * ((x + r + 1) % xn) + k
        for j in range(SUBS):
            go(remote(rows(f, v, j), rows(f, v, j), x_send.at[r, j], recv.at[r, 0, j], v, fo))
    own = remote(hid.at[f], hid.at[f], own_sems.at[0], own_sems.at[1], v, sib)
    go(own)
    loads[3].start()

    def src_of(r):
        return 2 * ((x + xn - r - 1) % xn) + k

    vd = vy + vz - v
    owners = (v, vy, vz, vd)

    def arrive(r, rel, j):
        fi = src_of(r)
        blk = rows(fi, owners[rel], j)
        remote(blk, blk, x_send.at[r, j], recv.at[r, rel, j], v, f).wait_recv()
        half = j < SUBS // 2
        if rel == 0:
            go(remote(blk, blk, y_send.at[r, 0, j], recv.at[r, 1, j], vy, f))
            go(remote(blk, blk, z_send.at[r, 0, j], recv.at[r, 2, j], vz, f))
        if rel == 1 and half:
            go(remote(blk, blk, z_send.at[r, 1, j], recv.at[r, 3, j], vz, f))
        if rel == 2 and not half:
            go(remote(blk, blk, y_send.at[r, 1, j], recv.at[r, 3, j], vy, f))
        go(remote(blk, blk, s_send.at[r, rel, j], s_recv.at[r, rel, j], v, sib))

    def post(send_buf, recv_buf, sends, recvs, d):
        @pl.when(d != me)
        def _():
            remote(send_buf, recv_buf, sends.at[d], recvs.at[me], d // nf, d % nf).start()

    o_t[...] = oproj[...].astype(F32).T.astype(BF16)
    base = me * vl

    def onehot_step(c, carry):
        ids = lax.broadcasted_iota(jnp.int32, (vl, tl), 0) + base
        hot = (targets[c] == ids).astype(F32).astype(BF16)
        o = jnp.dot(o_t[...], hot, preferred_element_type=F32)
        o_full[c] = o
        for b in range(bpc):
            for g in range(nf):
                d = (c * bpc + b) * nf + g
                so[d] = o[g * rf:(g + 1) * rf, b * tb:(b + 1) * tb].astype(BF16)
        for b in range(bpc):
            for g in range(nf):
                d = (c * bpc + b) * nf + g
                post(so.at[d], ro.at[me], so_send, ro_sem, d)
        return carry

    lax.fori_loop(0, nf, onehot_step, 0)

    vt = min(256, vl)
    nt = vl // vt

    def tiles(fi, lo, hi, m):
        def tile(i, m):
            at = pl.ds(pl.multiple_of(i * vt, vt), vt)
            l = lax.dot_general(head[at, :], hid[fi], NT, preferred_element_type=F32)
            lg[at, :] = l
            return jnp.maximum(m, jnp.max(l, axis=0, keepdims=True))
        return lax.fori_loop(lo, hi, tile, m)

    def finish(fi, m):
        e = jnp.exp(lg[...] - m)
        s = jnp.sum(e, axis=0, keepdims=True)
        u = jnp.dot(o_t[...], e.astype(BF16), preferred_element_type=F32)
        u = u / s - o_full[fi]
        for b in range(bpc):
            lanes = slice(b * tb, (b + 1) * tb)
            blk = fi * bpc + b
            st[blk, 0:1, :] = m[:, lanes]
            st[blk, 1:2, :] = s[:, lanes]
            for g in range(nf):
                sv[blk * nf + g] = u[g * rf:(g + 1) * rf, lanes].astype(BF16)
        for b in range(bpc):
            for g in range(nf):
                blk = fi * bpc + b
                d = blk * nf + g
                post(st.at[blk], rst.at[me], st_send, rst_sem, d)
                post(sv.at[d], rv.at[me], sv_send, rv_sem, d)
        ins[fi] = jnp.dot(hid[fi], iproj[...], preferred_element_type=F32)

    low = jnp.full((1, tl), -jnp.inf, F32)
    loads[1].wait()
    loads[2].wait()
    every = range(xn - 1)
    for r in every:
        arrive(r, 0, 0)
    m = tiles(f, 0, nt // 2, low)
    for r in every:
        arrive(r, 0, 1)
    m = tiles(f, nt // 2, nt, m)
    for r in every:
        arrive(r, 1, 0)
        arrive(r, 2, 0)
        arrive(r, 0, 2)
    finish(f, m)
    remote(hid.at[f], hid.at[sib], own_sems.at[0], own_sems.at[1], v, sib).wait_recv()
    m = tiles(sib, 0, nt // 2, low)
    for r in every:
        arrive(r, 1, 1)
        arrive(r, 2, 1)
        arrive(r, 0, 3)
    m = tiles(sib, nt // 2, nt, m)
    for r in every:
        arrive(r, 1, 2)
        arrive(r, 2, 2)
    finish(sib, m)
    for j in range(3, SUBS):
        for r in every:
            arrive(r, 1, j)
            arrive(r, 2, j)
    for j in range(SUBS):
        for r in every:
            arrive(r, 3, j)

    def remote_chunk(fi):
        finish(fi, tiles(fi, 0, nt, low))

    for r in every:
        remote_chunk(src_of(r))
    for r in every:
        fs = src_of(r) + 1 - 2 * k
        for rel in range(4):
            for j in range(SUBS):
                blk = rows(fs, owners[rel], j)
                remote(blk, blk, s_send.at[r, rel, j], s_recv.at[r, rel, j], v, sib).wait_recv()
        remote_chunk(fs)

    for a, b, i in ((sv, rv, 0), (so, ro, 1)):
        pltpu.make_async_copy(a.at[me], b.at[me], loc_sem.at[i]).start()
    pltpu.make_async_copy(st.at[v], rst.at[me], loc_sem.at[2]).start()
    for a, b, i in ((sv, rv, 0), (so, ro, 1)):
        pltpu.make_async_copy(a.at[me], b.at[me], loc_sem.at[i]).wait()
    pltpu.make_async_copy(st.at[v], rst.at[me], loc_sem.at[2]).wait()

    def take(p, c):
        d = (me + p) % nd
        remote(st.at[v], rst.at[d], st_send.at[d], rst_sem.at[d], v, f).wait_recv()
        remote(so.at[d], ro.at[d], so_send.at[d], ro_sem.at[d], v, f).wait_recv()
        remote(sv.at[d], rv.at[d], sv_send.at[d], rv_sem.at[d], v, f).wait_recv()
        return c

    lax.fori_loop(1, nd, take, 0)
    top = lax.fori_loop(0, nd, lambda d, t: jnp.maximum(t, rst[d, 0:1, :]), jnp.full((1, tb), -jnp.inf, F32))
    total = lax.fori_loop(
        0, nd, lambda d, t: t + jnp.exp(rst[d, 0:1, :] - top) * rst[d, 1:2, :], jnp.zeros((1, tb), F32))

    def add(d, acc):
        w = jnp.exp(rst[d, 0:1, :] - top) * rst[d, 1:2, :] / total
        return acc + w * rv[d].astype(F32) - (1.0 - w) * ro[d].astype(F32)

    osb[v] = lax.fori_loop(0, nd, add, jnp.zeros((rf, tb), F32))

    def spread(p, c):
        dv = (v + p) % nv
        remote(osb.at[v], osb.at[v], ag_send.at[p], ag_recv.at[v], dv, f).start()
        return c

    lax.fori_loop(1, nv, spread, 0)

    qg[...] = jnp.zeros_like(qg)

    def outer(p, c):
        b = (v + p) % nv

        @pl.when(p > 0)
        def _():
            remote(osb.at[b], osb.at[b], ag_send.at[p], ag_recv.at[b], v, f).wait_recv()

        member = (seqs[b] == lax.broadcasted_iota(jnp.int32, (SEQS, tb), 0)).astype(F32)
        o = osb[b]
        weighted = jnp.concatenate([member * o[i:i + 1, :] for i in range(rf)], axis=0)
        act = ins[b // bpc, pl.ds(pl.multiple_of((b % bpc) * tb, tb), tb), :]
        qg[...] += jnp.dot(weighted, act, preferred_element_type=F32, precision=lax.Precision.HIGHEST)
        return c

    lax.fori_loop(0, nv, outer, 0)
    for i in range(rf):
        qgm[:, i * rank:(i + 1) * rank] = qg[i * SEQS:(i + 1) * SEQS, :].astype(BF16)
    loads[3].wait()

    def score(p, c):
        g = (f + p) % nf
        part[g] = lax.dot_general(
            qgm[...], gs[pl.ds(pl.multiple_of(g * eo, eo), eo), :], NT, preferred_element_type=F32)

        @pl.when(p < nf)
        def _():
            remote(part.at[g], infl.at[f], in_send.at[p % nf], in_recv.at[f], v, g).start()
        return c

    lax.fori_loop(1, nf + 1, score, 0)
    result = part[f]
    for p in range(1, nf):
        g = (f + p) % nf
        remote(part.at[g], infl.at[g], in_send.at[p], in_recv.at[g], v, g).wait_recv()
        result = result + infl[g]
    out[...] = result

    for copy in pending:
        copy.wait_send()

    def drain(p, c):
        d = (me + p) % nd
        remote(st.at[d // nf], rst.at[me], st_send.at[d], rst_sem.at[me], v, f).wait_send()
        remote(so.at[d], ro.at[me], so_send.at[d], ro_sem.at[me], v, f).wait_send()
        remote(sv.at[d], rv.at[me], sv_send.at[d], rv_sem.at[me], v, f).wait_send()
        return c

    lax.fori_loop(1, nd, drain, 0)
    for p in range(1, nv):
        remote(osb.at[v], osb.at[v], ag_send.at[p], ag_recv.at[v], v, f).wait_send()
    for p in range(1, nf):
        g = (f + p) % nf
        remote(part.at[g], infl.at[f], in_send.at[p], in_recv.at[f], v, f).wait_send()


def solution(mesh):
    nv, nf = mesh.shape["vocab"], mesh.shape["feat"]
    nd = nv * nf
    xn = nf // 2

    def on_device(hidden, out_head, out_proj, in_proj, targets, seq_ids, grad_store):
        tl, width = hidden.shape
        vl, rank = out_proj.shape
        el, fl = grad_store.shape
        tokens = tl * nf
        rf, tb, eo = rank // nf, tokens // nv, el // nf
        any_spec = pl.BlockSpec(memory_space=pl.ANY)
        vmem = pl.BlockSpec(memory_space=pltpu.VMEM)
        dma = pltpu.SemaphoreType.DMA
        res = pl.pallas_call(
            functools.partial(kernel, nv, nf),
            out_shape=jax.ShapeDtypeStruct((SEQS, eo), F32),
            in_specs=[any_spec, any_spec, vmem, any_spec, vmem, vmem, any_spec],
            out_specs=vmem,
            scratch_shapes=[
                pltpu.VMEM((nf, tl, width), BF16),
                pltpu.VMEM((vl, width), BF16),
                pltpu.VMEM((width, rank), BF16),
                pltpu.VMEM((el, fl), BF16),
                pltpu.VMEM((vl, tl), F32),
                pltpu.VMEM((rank, vl), BF16),
                pltpu.VMEM((nf, rank, tl), F32),
                pltpu.VMEM((nf, tl, rank), F32),
                pltpu.VMEM((nd, rf, tb), BF16),
                pltpu.VMEM((nd, rf, tb), BF16),
                pltpu.VMEM((nv, 8, tb), F32),
                pltpu.VMEM((nd, rf, tb), BF16),
                pltpu.VMEM((nd, rf, tb), BF16),
                pltpu.VMEM((nd, 8, tb), F32),
                pltpu.VMEM((nv, rf, tb), F32),
                pltpu.VMEM((rf * SEQS, rank), F32),
                pltpu.VMEM((SEQS, fl), BF16),
                pltpu.VMEM((nf, SEQS, eo), F32),
                pltpu.VMEM((nf, SEQS, eo), F32),
                dma((4,)),
                dma((xn - 1, SUBS)),
                dma((xn - 1, 2, SUBS)),
                dma((xn - 1, 2, SUBS)),
                dma((xn - 1, 4, SUBS)),
                dma((xn - 1, 4, SUBS)),
                dma((xn - 1, 4, SUBS)),
                dma((2,)),
                dma((nd,)),
                dma((nd,)),
                dma((nd,)),
                dma((nd,)),
                dma((nd,)),
                dma((nd,)),
                dma((nv,)),
                dma((nv,)),
                dma((nf,)),
                dma((nf,)),
                dma((3,)),
            ],
            compiler_params=pltpu.CompilerParams(
                collective_id=0, has_side_effects=True, vmem_limit_bytes=60 * 1024 * 1024),
        )(hidden, out_head, out_proj, in_proj, targets.reshape(nf, 1, tl), seq_ids.reshape(nv, 1, tb), grad_store)
        return res.T

    in_specs = (
        P("feat", None),
        P(("vocab", "feat"), None),
        P(("vocab", "feat"), None),
        P(),
        P(),
        P(),
        P("vocab", "feat"),
    )
    return jax.shard_map(
        on_device, mesh=mesh, in_specs=in_specs, out_specs=P(("vocab", "feat"), None), check_vma=False
    )
```

time: 307 us -> 72.2 us (0.24)
  waiting for transfers between devices: 172 us -> 0 us
  blocking collectives: 80.3 us -> 0 us
  Pallas kernels: 0 us -> 70.1 us
  matrix products: 37.7 us -> 0 us
  between operations: 13.2 us -> 0.01 us
  other arithmetic: 3.97 us -> 0 us
    pallas_call x0 -> x1, Pallas kernels: none -> 70.1 us  [on_device(): pl.pallas_call(functools.partial(kernel, nv, nf), out_shape=jax.ShapeDtyp...]
    psum x1 -> x0, waiting for transfers between devices: 67.8 us -> none  [on_device(): out_part = lax.psum(feat_cols, 'vocab')]
    all_gather x1 -> x0, waiting for transfers between devices: 62.6 us -> none  [on_device(): tok_piece = lax.all_gather(hidden, 'feat', axis=0, tiled=True)]
    psum x1 -> x0, blocking collectives: 41 us -> none  [on_device(): global_sum = lax.psum(jnp.sum(expval, axis=1), ('vocab', 'feat'))]
    reduce_scatter x2 -> x0, waiting for transfers between devices: 40.4 us -> none  [the longest x1 21.5 us: on_device(): lax.psum_scatter(partial_out, 'feat', scatter_dimension=1, tiled=True)]
    pmax x1 -> x0, blocking collectives: 39.3 us -> none  [on_device(): global_max = lax.pmax(local_max, ('vocab', 'feat'))]
    dot_general x5 -> x0, matrix products: 37.7 us -> none  [the longest x1 15 us: on_device(): lax.dot_general(tok_piece, out_head, (((1,), (1,)), ((), ())), preferred_...]
  transfers between devices with their start and end apart: 4 -> 0, of which waited for: 4 -> 0; matrix products, arithmetic and copies ran while one was open for 2% -> 0% of each run, Pallas kernels for 0% -> 0%
where the time goes in v1:
time: 72.2 us; the launch traced here: 71.5 us
  Pallas kernels  70.1 us (97%)
  local copies, waits for them, and re-layouts  1.38 us (2%)
    pallas_call x1, Pallas kernels, on_device(): pl.pallas_call(functools.partial(kernel, nv, nf), out_shape=jax.ShapeDtyp...  70.1 us

profile of v1, /device:TPU:0, one launch (start us, length us, event | category | flops | bytes accessed | tf_op | source)
XLA Modules:
  0.0 71.5 jit_solution(1637250440180301722)
XLA Ops:
  0.0 70.1 %shard_map.73 = f32[16,512]{1,0:T(8,128)} custom-call(bf16[256,4096]{1,0:T(8,128)(2,1)} %hid_in.1, bf16[1024,4096]{1,0:T(8,128)(2,1)} %head_in.1, bf16[1024,128]{1,0:T(8,128)(2,1)} %oproj.1, bf16[4096,128]{1,0:T(8,128)(2,1)} %iproj_in.1, s32[4,1,256]{2,1,0:T(1,128)} %bitcast.4, s32[8,1,128]{2,1,0:T(1,128)} %bitcast.5, bf16[2048,4096]{1,0:T(8,128)(2,1)} %gs_in.1), custom_call_target="tpu_custom_call" | custom-call | tf_op jit(solution)/shard_map/pallas_call | solution.py:309
  70.1 1.4 %copy.9 = f32[512,16]{0,1:T(8,128)} copy(f32[512,16]{0,1:T(8,128)} %bitcast.3) | data formatting | bytes 65536

commit v2 on v1

v2 whole, which is shorter than its diff:
```python
import functools

import jax
import jax.numpy as jnp
from jax import lax
from jax.experimental import pallas as pl
from jax.experimental.pallas import tpu as pltpu
from jax.sharding import PartitionSpec as P

SEQS = 16
SUBS = 4
F32 = jnp.float32
BF16 = jnp.bfloat16
NT = (((1,), (1,)), ((), ()))


def kernel(nv, nf, hid_in, head_in, oproj, iproj_in, targets, seqs, gs_in, out,
           hid, head, iproj, gs, lg, o_t, o_full, ins, sv, so, st, rv, ro, rst, osb, qg, qgm, part, infl,
           load_sem, x_send, y_send, z_send, s_send, recv, s_recv, own_sems,
           sv_send, so_send, st_send, rv_sem, ro_sem, rst_sem, ag_send, ag_recv, in_send, in_recv, loc_sem):
    v = lax.axis_index("vocab")
    f = lax.axis_index("feat")
    me = v * nf + f
    nd = nv * nf
    x, k = f // 2, f % 2
    xn = nf // 2
    sib = f + 1 - 2 * k
    vy = v + 1 - 2 * (v % 2)
    vz = v + 2 - 4 * ((v // 2) % 2)
    vl = head.shape[0]
    rank = oproj.shape[1]
    rf, tb = sv.shape[1], sv.shape[2]
    parts = hid.shape[1]
    tc = 2 * tb
    eo = out.shape[1]
    piece = tb // 4
    per = SUBS // parts
    sr = piece // per

    loads = [
        pltpu.make_async_copy(head_in, head, load_sem.at[0]),
        pltpu.make_async_copy(iproj_in, iproj, load_sem.at[1]),
        pltpu.make_async_copy(gs_in, gs, load_sem.at[2]),
    ]

    def half(xi, kk, h):
        return hid.at[xi, h, pl.ds(pl.multiple_of(kk * tb, tb), tb)]

    mine = [pltpu.make_async_copy(hid_in.at[pl.ds(h * tb, tb)], half(x, k, h), load_sem.at[3 + h])
            for h in range(parts)]
    for copy in mine + loads[:2]:
        copy.start()

    barrier = pltpu.get_barrier_semaphore()

    def greet(p, c):
        d = (me + p) % nd
        pl.semaphore_signal(barrier, inc=1, device_id={"vocab": d // nf, "feat": d % nf},
                            device_id_type=pl.DeviceIdType.MESH)
        return c

    lax.fori_loop(1, nd, greet, 0)
    pl.semaphore_wait(barrier, nd - 1)

    def remote(src, dst, ss, rs, dv, df):
        return pltpu.make_async_remote_copy(
            src_ref=src, dst_ref=dst, send_sem=ss, recv_sem=rs,
            device_id={"vocab": dv, "feat": df}, device_id_type=pl.DeviceIdType.MESH)

    def rows(xi, kk, owner, j):
        at = kk * tb + (owner % 4) * piece + (j % per) * sr
        return hid.at[xi, j // per, pl.ds(pl.multiple_of(at, sr), sr)]

    pending = []

    def go(copy):
        copy.start()
        pending.append(copy)

    for h in range(parts):
        mine[h].wait()
        for r in range(xn - 1):
            fo = 2 * ((x + r + 1) % xn) + k
            for j in range(h * per, (h + 1) * per):
                blk = rows(x, k, v, j)
                go(remote(blk, blk, x_send.at[r, j], recv.at[r, 0, j], v, fo))
        go(remote(half(x, k, h), half(x, k, h), own_sems.at[0, h], own_sems.at[1, h], v, sib))
    loads[2].start()

    def src_of(r):
        return (x + xn - r - 1) % xn

    vd = vy + vz - v
    owners = (v, vy, vz, vd)

    def arrive(r, rel, j):
        blk = rows(src_of(r), k, owners[rel], j)
        remote(blk, blk, x_send.at[r, j], recv.at[r, rel, j], v, f).wait_recv()
        first = j % per < per // 2
        if rel == 0:
            go(remote(blk, blk, y_send.at[r, 0, j], recv.at[r, 1, j], vy, f))
            go(remote(blk, blk, z_send.at[r, 0, j], recv.at[r, 2, j], vz, f))
        if rel == 1 and first:
            go(remote(blk, blk, z_send.at[r, 1, j], recv.at[r, 3, j], vz, f))
        if rel == 2 and not first:
            go(remote(blk, blk, y_send.at[r, 1, j], recv.at[r, 3, j], vy, f))
        go(remote(blk, blk, s_send.at[r, rel, j], s_recv.at[r, rel, j], v, sib))

    def post(send_buf, recv_buf, sends, recvs, d):
        @pl.when(d != me)
        def _():
            remote(send_buf, recv_buf, sends.at[d], recvs.at[me], d // nf, d % nf).start()

    o_t[...] = oproj[...].astype(F32).T.astype(BF16)
    base = me * vl

    def onehot_step(c, carry):
        xi, h = c // parts, c % parts
        blks = [(2 * xi + kk) * parts + h for kk in range(2)]
        ids = lax.broadcasted_iota(jnp.int32, (vl, tc), 0) + base
        goal = jnp.concatenate([targets[b] for b in blks], axis=1)
        hot = (goal == ids).astype(F32).astype(BF16)
        o = jnp.dot(o_t[...], hot, preferred_element_type=F32)
        o_full[c] = o
        for kk in range(2):
            for g in range(nf):
                so[blks[kk] * nf + g] = o[g * rf:(g + 1) * rf, kk * tb:(kk + 1) * tb].astype(BF16)
        for kk in range(2):
            for g in range(nf):
                d = blks[kk] * nf + g
                post(so.at[d], ro.at[me], so_send, ro_sem, d)
        return carry

    lax.fori_loop(0, xn * parts, onehot_step, 0)

    vt = min(256, vl)
    nt = vl // vt

    def tiles(xi, h, lo, hi, m):
        def tile(i, m):
            at = pl.ds(pl.multiple_of(i * vt, vt), vt)
            l = lax.dot_general(head[at, :], hid[xi, h], NT, preferred_element_type=F32)
            lg[at, :] = l
            return jnp.maximum(m, jnp.max(l, axis=0, keepdims=True))
        return lax.fori_loop(lo, hi, tile, m)

    def finish(xi, h, m):
        e = jnp.exp(lg[...] - m)
        s = jnp.sum(e, axis=0, keepdims=True)
        u = jnp.dot(o_t[...], e.astype(BF16), preferred_element_type=F32)
        u = u / s - o_full[xi * parts + h]
        blks = [(2 * xi + kk) * parts + h for kk in range(2)]
        for kk in range(2):
            lanes = slice(kk * tb, (kk + 1) * tb)
            st[blks[kk], 0:1, :] = m[:, lanes]
            st[blks[kk], 1:2, :] = s[:, lanes]
            for g in range(nf):
                sv[blks[kk] * nf + g] = u[g * rf:(g + 1) * rf, lanes].astype(BF16)
        for kk in range(2):
            for g in range(nf):
                d = blks[kk] * nf + g
                post(st.at[blks[kk]], rst.at[me], st_send, rst_sem, d)
                post(sv.at[d], rv.at[me], sv_send, rv_sem, d)
        act = jnp.dot(hid[xi, h], iproj[...], preferred_element_type=F32)
        for kk in range(2):
            ins[blks[kk]] = act[kk * tb:(kk + 1) * tb]

    low = jnp.full((1, tc), -jnp.inf, F32)
    every = range(xn - 1)

    def sibling(h):
        blk = half(x, 1 - k, h)
        remote(blk, blk, own_sems.at[0, h], own_sems.at[1, h], v, sib).wait_recv()

    def arrivals(*which):
        for rel, j in which:
            for r in every:
                arrive(r, rel, j)

    def passed(r, h):
        for rel in range(4):
            for j in range(h * per, (h + 1) * per):
                blk = rows(src_of(r), 1 - k, owners[rel], j)
                remote(blk, blk, s_send.at[r, rel, j], s_recv.at[r, rel, j], v, sib).wait_recv()

    mid = nt // 2
    loads[0].wait()
    loads[1].wait()
    sibling(0)
    arrivals((0, 0))
    m = tiles(x, 0, 0, mid, low)
    arrivals((0, 1))
    m = tiles(x, 0, mid, nt, m)
    arrivals((1, 0), (2, 0), (0, 2))
    finish(x, 0, m)
    sibling(1)
    m = tiles(x, 1, 0, mid, low)
    arrivals((1, 1), (2, 1), (0, 3))
    m = tiles(x, 1, mid, nt, m)
    finish(x, 1, m)
    arrivals((3, 0), (3, 1))
    for r in every:
        passed(r, 0)
        m = tiles(src_of(r), 0, 0, mid, low)
        if r == 0:
            arrivals((1, 2), (2, 2))
        m = tiles(src_of(r), 0, mid, nt, m)
        finish(src_of(r), 0, m)
    arrivals((1, 3), (2, 3), (3, 2), (3, 3))
    for r in every:
        passed(r, 1)
        finish(src_of(r), 1, tiles(src_of(r), 1, 0, nt, low))

    for a, b, i in ((sv, rv, 0), (so, ro, 1)):
        pltpu.make_async_copy(a.at[me], b.at[me], loc_sem.at[i]).start()
    pltpu.make_async_copy(st.at[v], rst.at[me], loc_sem.at[2]).start()
    for a, b, i in ((sv, rv, 0), (so, ro, 1)):
        pltpu.make_async_copy(a.at[me], b.at[me], loc_sem.at[i]).wait()
    pltpu.make_async_copy(st.at[v], rst.at[me], loc_sem.at[2]).wait()

    def take(p, c):
        d = (me + p) % nd
        remote(st.at[v], rst.at[d], st_send.at[d], rst_sem.at[d], v, f).wait_recv()
        remote(so.at[d], ro.at[d], so_send.at[d], ro_sem.at[d], v, f).wait_recv()
        remote(sv.at[d], rv.at[d], sv_send.at[d], rv_sem.at[d], v, f).wait_recv()
        return c

    lax.fori_loop(1, nd, take, 0)
    peak, mass = rst[:, 0, :], rst[:, 1, :]
    mass = jnp.exp(peak - jnp.max(peak, axis=0, keepdims=True)) * mass
    share = mass / jnp.sum(mass, axis=0, keepdims=True)
    acc = jnp.zeros((rf, tb), F32)
    for d in range(nd):
        w = share[d:d + 1, :]
        acc = acc + w * rv[d].astype(F32) - (1.0 - w) * ro[d].astype(F32)
    osb[v] = acc

    def spread(p, c):
        dv = (v + p) % nv
        remote(osb.at[v], osb.at[v], ag_send.at[p], ag_recv.at[v], dv, f).start()
        return c

    lax.fori_loop(1, nv, spread, 0)

    qg[...] = jnp.zeros_like(qg)

    def outer(p, c):
        b = (v + p) % nv

        @pl.when(p > 0)
        def _():
            remote(osb.at[b], osb.at[b], ag_send.at[p], ag_recv.at[b], v, f).wait_recv()

        member = (seqs[b] == lax.broadcasted_iota(jnp.int32, (SEQS, tb), 0)).astype(F32)
        o = osb[b]
        weighted = jnp.concatenate([member * o[i:i + 1, :] for i in range(rf)], axis=0)
        qg[...] += jnp.dot(weighted, ins[b], preferred_element_type=F32, precision=lax.Precision.HIGHEST)
        return c

    lax.fori_loop(0, nv, outer, 0)
    for i in range(rf):
        qgm[:, i * rank:(i + 1) * rank] = qg[i * SEQS:(i + 1) * SEQS, :].astype(BF16)
    loads[2].wait()

    def score(p, c):
        g = (f + p) % nf
        part[g] = lax.dot_general(
            qgm[...], gs[pl.ds(pl.multiple_of(g * eo, eo), eo), :], NT, preferred_element_type=F32)

        @pl.when(p < nf)
        def _():
            remote(part.at[g], infl.at[f], in_send.at[p % nf], in_recv.at[f], v, g).start()
        return c

    lax.fori_loop(1, nf + 1, score, 0)
    result = part[f]
    for p in range(1, nf):
        g = (f + p) % nf
        remote(part.at[g], infl.at[g], in_send.at[p], in_recv.at[g], v, g).wait_recv()
        result = result + infl[g]
    out[...] = result

    for copy in pending:
        copy.wait_send()

    def drain(p, c):
        d = (me + p) % nd
        remote(st.at[d // nf], rst.at[me], st_send.at[d], rst_sem.at[me], v, f).wait_send()
        remote(so.at[d], ro.at[me], so_send.at[d], ro_sem.at[me], v, f).wait_send()
        remote(sv.at[d], rv.at[me], sv_send.at[d], rv_sem.at[me], v, f).wait_send()
        return c

    lax.fori_loop(1, nd, drain, 0)
    for p in range(1, nv):
        remote(osb.at[v], osb.at[v], ag_send.at[p], ag_recv.at[v], v, f).wait_send()
    for p in range(1, nf):
        g = (f + p) % nf
        remote(part.at[g], infl.at[f], in_send.at[p], in_recv.at[f], v, f).wait_send()


def solution(mesh):
    nv, nf = mesh.shape["vocab"], mesh.shape["feat"]
    nd = nv * nf
    xn = nf // 2

    def on_device(hidden, out_head, out_proj, in_proj, targets, seq_ids, grad_store):
        tl, width = hidden.shape
        vl, rank = out_proj.shape
        el, fl = grad_store.shape
        tokens = tl * nf
        rf, tb, eo = rank // nf, tokens // nv, el // nf
        parts = tl // tb
        any_spec = pl.BlockSpec(memory_space=pl.ANY)
        vmem = pl.BlockSpec(memory_space=pltpu.VMEM)
        dma = pltpu.SemaphoreType.DMA
        res = pl.pallas_call(
            functools.partial(kernel, nv, nf),
            out_shape=jax.ShapeDtypeStruct((SEQS, eo), F32),
            in_specs=[any_spec, any_spec, vmem, any_spec, vmem, vmem, any_spec],
            out_specs=vmem,
            scratch_shapes=[
                pltpu.VMEM((xn, parts, 2 * tb, width), BF16),
                pltpu.VMEM((vl, width), BF16),
                pltpu.VMEM((width, rank), BF16),
                pltpu.VMEM((el, fl), BF16),
                pltpu.VMEM((vl, 2 * tb), F32),
                pltpu.VMEM((rank, vl), BF16),
                pltpu.VMEM((xn * parts, rank, 2 * tb), F32),
                pltpu.VMEM((nv, tb, rank), F32),
                pltpu.VMEM((nd, rf, tb), BF16),
                pltpu.VMEM((nd, rf, tb), BF16),
                pltpu.VMEM((nv, 8, tb), F32),
                pltpu.VMEM((nd, rf, tb), BF16),
                pltpu.VMEM((nd, rf, tb), BF16),
                pltpu.VMEM((nd, 8, tb), F32),
                pltpu.VMEM((nv, rf, tb), F32),
                pltpu.VMEM((rf * SEQS, rank), F32),
                pltpu.VMEM((SEQS, fl), BF16),
                pltpu.VMEM((nf, SEQS, eo), F32),
                pltpu.VMEM((nf, SEQS, eo), F32),
                dma((3 + parts,)),
                dma((xn - 1, SUBS)),
                dma((xn - 1, 2, SUBS)),
                dma((xn - 1, 2, SUBS)),
                dma((xn - 1, 4, SUBS)),
                dma((xn - 1, 4, SUBS)),
                dma((xn - 1, 4, SUBS)),
                dma((2, parts)),
                dma((nd,)),
                dma((nd,)),
                dma((nd,)),
                dma((nd,)),
                dma((nd,)),
                dma((nd,)),
                dma((nv,)),
                dma((nv,)),
                dma((nf,)),
                dma((nf,)),
                dma((3,)),
            ],
            compiler_params=pltpu.CompilerParams(
                collective_id=0, has_side_effects=True, vmem_limit_bytes=60 * 1024 * 1024),
        )(hidden, out_head, out_proj, in_proj, targets.reshape(nv, 1, tb), seq_ids.reshape(nv, 1, tb), grad_store)
        return res.T

    in_specs = (
        P("feat", None),
        P(("vocab", "feat"), None),
        P(("vocab", "feat"), None),
        P(),
        P(),
        P(),
        P("vocab", "feat"),
    )
    return jax.shard_map(
        on_device, mesh=mesh, in_specs=in_specs, out_specs=P(("vocab", "feat"), None), check_vma=False
    )
```

time: 72.2 us -> 70 us (0.970)
  Pallas kernels: 70.1 us -> 67.9 us
    pallas_call x1, Pallas kernels: 70.1 us -> 67.9 us  [on_device(): pl.pallas_call(functools.partial(kernel, nv, nf), out_shape=jax.ShapeDtyp...]
where the time goes in v2:
time: 70 us; the launch traced here: 69.2 us
  Pallas kernels  67.9 us (97%)
  local copies, waits for them, and re-layouts  1.38 us (2%)
    pallas_call x1, Pallas kernels, on_device(): pl.pallas_call(functools.partial(kernel, nv, nf), out_shape=jax.ShapeDtyp...  67.9 us

profile of v2, /device:TPU:0, one launch (start us, length us, event | category | flops | bytes accessed | tf_op | source)
XLA Modules:
  0.0 69.2 jit_solution(14349906958307133000)
XLA Ops:
  0.0 67.9 %shard_map.73 = f32[16,512]{1,0:T(8,128)} custom-call(bf16[256,4096]{1,0:T(8,128)(2,1)} %hid_in.1, bf16[1024,4096]{1,0:T(8,128)(2,1)} %head_in.1, bf16[1024,128]{1,0:T(8,128)(2,1)} %oproj.1, bf16[4096,128]{1,0:T(8,128)(2,1)} %iproj_in.1, s32[8,1,128]{2,1,0:T(1,128)} %bitcast.4, s32[8,1,128]{2,1,0:T(1,128)} %bitcast.5, bf16[2048,4096]{1,0:T(8,128)(2,1)} %gs_in.1), custom_call_target="tpu_custom_call" | custom-call | tf_op jit(solution)/shard_map/pallas_call | solution.py:316
  67.9 1.4 %copy.9 = f32[512,16]{0,1:T(8,128)} copy(f32[512,16]{0,1:T(8,128)} %bitcast.3) | data formatting | bytes 65536

commit v3 on v2

--- a/solution.py
+++ b/solution.py
@@ -15,9 +15,9 @@
 
 
 def kernel(nv, nf, hid_in, head_in, oproj, iproj_in, targets, seqs, gs_in, out,
-           hid, head, iproj, gs, lg, o_t, o_full, ins, sv, so, st, rv, ro, rst, osb, qg, qgm, part, infl,
+           hid, head, iproj, gs, lg, o_t, o_full, ins, sv, so, s2, st, rv, r1, ro, rst, osb, qg, qgm, part, infl,
            load_sem, x_send, y_send, z_send, s_send, recv, s_recv, own_sems,
-           sv_send, so_send, st_send, rv_sem, ro_sem, rst_sem, ag_send, ag_recv, in_send, in_recv, loc_sem):
+           sv_send, so_send, s2_send, st_send, rv_sem, r1_sem, ro_sem, rst_sem, ag_send, ag_recv, in_send, in_recv, loc_sem, heard):
     v = lax.axis_index("vocab")
     f = lax.axis_index("feat")
     me = v * nf + f
@@ -51,16 +51,27 @@
     for copy in mine + loads[:2]:
         copy.start()
 
+    def flip(i, bit):
+        return i + bit - 2 * bit * ((i // bit) % 2)
+
+    near = [(v, flip(f, 1 << i)) for i in range(nf.bit_length() - 1)]
+    near += [(flip(v, 1 << i), f) for i in range(nv.bit_length() - 1)]
     barrier = pltpu.get_barrier_semaphore()
 
-    def greet(p, c):
-        d = (me + p) % nd
-        pl.semaphore_signal(barrier, inc=1, device_id={"vocab": d // nf, "feat": d % nf},
+    def signal(sem, place):
+        pl.semaphore_signal(sem, inc=1, device_id={"vocab": place[0], "feat": place[1]},
                             device_id_type=pl.DeviceIdType.MESH)
-        return c
-
-    lax.fori_loop(1, nd, greet, 0)
-    pl.semaphore_wait(barrier, nd - 1)
+
+    for place in near:
+        signal(barrier, place)
+    pl.semaphore_wait(barrier, len(near))
+
+    def hear(lo, hi):
+        for i in range(lo, hi):
+            signal(heard.at[i], near[i])
+            pl.semaphore_wait(heard.at[i], 1)
+
+    hear(0, nf.bit_length() - 1)
 
     def remote(src, dst, ss, rs, dv, df):
         return pltpu.make_async_remote_copy(
@@ -124,14 +135,31 @@
         o_full[c] = o
         for kk in range(2):
             for g in range(nf):
-                so[blks[kk] * nf + g] = o[g * rf:(g + 1) * rf, kk * tb:(kk + 1) * tb].astype(BF16)
-        for kk in range(2):
-            for g in range(nf):
-                d = blks[kk] * nf + g
-                post(so.at[d], ro.at[me], so_send, ro_sem, d)
+                so[g, blks[kk]] = o[g * rf:(g + 1) * rf, kk * tb:(kk + 1) * tb].astype(BF16)
         return carry
 
     lax.fori_loop(0, xn * parts, onehot_step, 0)
+    hear(nf.bit_length() - 1, len(near))
+    for p in range(1, nf):
+        g = (f + p) % nf
+        go(remote(so.at[g], r1.at[f], so_send.at[p], r1_sem.at[f], v, g))
+
+    def onehot_sum():
+        for p in range(1, nf):
+            g = (f + p) % nf
+            remote(so.at[g], r1.at[g], so_send.at[p], r1_sem.at[g], v, g).wait_recv()
+
+        def one(b, c):
+            t = so[f, b].astype(F32)
+            for p in range(1, nf):
+                t = t + r1[(f + p) % nf, b].astype(F32)
+            s2[b] = t.astype(BF16)
+            return c
+
+        lax.fori_loop(0, nv, one, 0)
+        for p in range(1, nv):
+            b = (v + p) % nv
+            go(remote(s2.at[b], ro.at[v], s2_send.at[p], ro_sem.at[v], b, f))
 
     vt = min(256, vl)
     nt = vl // vt
@@ -198,6 +226,7 @@
     arrivals((1, 1), (2, 1), (0, 3))
     m = tiles(x, 1, mid, nt, m)
     finish(x, 1, m)
+    onehot_sum()
     arrivals((3, 0), (3, 1))
     for r in every:
         passed(r, 0)
@@ -211,17 +240,21 @@
         passed(r, 1)
         finish(src_of(r), 1, tiles(src_of(r), 1, 0, nt, low))
 
-    for a, b, i in ((sv, rv, 0), (so, ro, 1)):
-        pltpu.make_async_copy(a.at[me], b.at[me], loc_sem.at[i]).start()
-    pltpu.make_async_copy(st.at[v], rst.at[me], loc_sem.at[2]).start()
-    for a, b, i in ((sv, rv, 0), (so, ro, 1)):
-        pltpu.make_async_copy(a.at[me], b.at[me], loc_sem.at[i]).wait()
-    pltpu.make_async_copy(st.at[v], rst.at[me], loc_sem.at[2]).wait()
+    local = [pltpu.make_async_copy(sv.at[me], rv.at[me], loc_sem.at[0]),
+             pltpu.make_async_copy(st.at[v], rst.at[me], loc_sem.at[1])]
+    for copy in local:
+        copy.start()
+    targeted = s2[v].astype(F32)
+    for p in range(1, nv):
+        b = (v + p) % nv
+        remote(s2.at[b], ro.at[b], s2_send.at[p], ro_sem.at[b], v, f).wait_recv()
+        targeted = targeted + ro[b].astype(F32)
+    for copy in local:
+        copy.wait()
 
     def take(p, c):
         d = (me + p) % nd
         remote(st.at[v], rst.at[d], st_send.at[d], rst_sem.at[d], v, f).wait_recv()
-        remote(so.at[d], ro.at[d], so_send.at[d], ro_sem.at[d], v, f).wait_recv()
         remote(sv.at[d], rv.at[d], sv_send.at[d], rv_sem.at[d], v, f).wait_recv()
         return c
 
@@ -229,10 +262,13 @@
     peak, mass = rst[:, 0, :], rst[:, 1, :]
     mass = jnp.exp(peak - jnp.max(peak, axis=0, keepdims=True)) * mass
     share = mass / jnp.sum(mass, axis=0, keepdims=True)
-    acc = jnp.zeros((rf, tb), F32)
+    first_row = lax.broadcasted_iota(jnp.int32, (nd, tb), 0) * vl
+    goal = targets[v]
+    outside = (goal < first_row) | (goal >= first_row + vl)
+    acc = -jnp.sum(jnp.where(outside, share, 0.0), axis=0, keepdims=True) * targeted
     for d in range(nd):
         w = share[d:d + 1, :]
-        acc = acc + w * rv[d].astype(F32) - (1.0 - w) * ro[d].astype(F32)
+        acc = acc + w * rv[d].astype(F32)
     osb[v] = acc
 
     def spread(p, c):
@@ -286,7 +322,6 @@
     def drain(p, c):
         d = (me + p) % nd
         remote(st.at[d // nf], rst.at[me], st_send.at[d], rst_sem.at[me], v, f).wait_send()
-        remote(so.at[d], ro.at[me], so_send.at[d], ro_sem.at[me], v, f).wait_send()
         remote(sv.at[d], rv.at[me], sv_send.at[d], rv_sem.at[me], v, f).wait_send()
         return c
 
@@ -328,11 +363,13 @@
                 pltpu.VMEM((xn * parts, rank, 2 * tb), F32),
                 pltpu.VMEM((nv, tb, rank), F32),
                 pltpu.VMEM((nd, rf, tb), BF16),
+                pltpu.VMEM((nf, nv, rf, tb), BF16),
+                pltpu.VMEM((nv, rf, tb), BF16),
+                pltpu.VMEM((nv, 2, tb), F32),
                 pltpu.VMEM((nd, rf, tb), BF16),
-                pltpu.VMEM((nv, 8, tb), F32),
-                pltpu.VMEM((nd, rf, tb), BF16),
-                pltpu.VMEM((nd, rf, tb), BF16),
-                pltpu.VMEM((nd, 8, tb), F32),
+                pltpu.VMEM((nf, nv, rf, tb), BF16),
+                pltpu.VMEM((nv, rf, tb), BF16),
+                pltpu.VMEM((nd, 2, tb), F32),
                 pltpu.VMEM((nv, rf, tb), F32),
                 pltpu.VMEM((rf * SEQS, rank), F32),
                 pltpu.VMEM((SEQS, fl), BF16),
@@ -347,16 +384,19 @@
                 dma((xn - 1, 4, SUBS)),
                 dma((2, parts)),
                 dma((nd,)),
+                dma((nf,)),
+                dma((nv,)),
                 dma((nd,)),
                 dma((nd,)),
-                dma((nd,)),
-                dma((nd,)),
+                dma((nf,)),
+                dma((nv,)),
                 dma((nd,)),
                 dma((nv,)),
                 dma((nv,)),
                 dma((nf,)),
                 dma((nf,)),
-                dma((3,)),
+                dma((2,)),
+                pltpu.SemaphoreType.REGULAR((nf.bit_length() + nv.bit_length() - 2,)),
             ],
             compiler_params=pltpu.CompilerParams(
                 collective_id=0, has_side_effects=True, vmem_limit_bytes=60 * 1024 * 1024),

time: 70 us -> 65.1 us (0.930)
  Pallas kernels: 67.9 us -> 63 us
    pallas_call x1, Pallas kernels: 67.9 us -> 63 us  [on_device(): pl.pallas_call(functools.partial(kernel, nv, nf), out_shape=jax.ShapeDtyp...]
where the time goes in v3:
time: 65.1 us; the launch traced here: 64.4 us
  Pallas kernels  63 us (97%)
  local copies, waits for them, and re-layouts  1.38 us (2%)
    pallas_call x1, Pallas kernels, on_device(): pl.pallas_call(functools.partial(kernel, nv, nf), out_shape=jax.ShapeDtyp...  63 us
    unnamed x1, local copies, waits for them, and re-layouts  1.38 us

profile of v3, /device:TPU:0, one launch (start us, length us, event | category | flops | bytes accessed | tf_op | source)
XLA Modules:
  0.0 64.4 jit_solution(14618450583687183113)
XLA Ops:
  0.0 63.0 %shard_map.73 = f32[16,512]{1,0:T(8,128)} custom-call(bf16[256,4096]{1,0:T(8,128)(2,1)} %hid_in.1, bf16[1024,4096]{1,0:T(8,128)(2,1)} %head_in.1, bf16[1024,128]{1,0:T(8,128)(2,1)} %oproj.1, bf16[4096,128]{1,0:T(8,128)(2,1)} %iproj_in.1, s32[8,1,128]{2,1,0:T(1,128)} %bitcast.4, s32[8,1,128]{2,1,0:T(1,128)} %bitcast.5, bf16[2048,4096]{1,0:T(8,128)(2,1)} %gs_in.1), custom_call_target="tpu_custom_call" | custom-call | tf_op jit(solution)/shard_map/pallas_call | solution.py:351
  63.0 1.4 %copy.9 = f32[512,16]{0,1:T(8,128)} copy(f32[512,16]{0,1:T(8,128)} %bitcast.3) | data formatting | bytes 65536

commit v4 on v3

--- a/solution.py
+++ b/solution.py
@@ -27,6 +27,7 @@
     sib = f + 1 - 2 * k
     vy = v + 1 - 2 * (v % 2)
     vz = v + 2 - 4 * ((v // 2) % 2)
+    vd = vy + vz - v
     vl = head.shape[0]
     rank = oproj.shape[1]
     rf, tb = sv.shape[1], sv.shape[2]
@@ -95,25 +96,31 @@
             for j in range(h * per, (h + 1) * per):
                 blk = rows(x, k, v, j)
                 go(remote(blk, blk, x_send.at[r, j], recv.at[r, 0, j], v, fo))
+        if h == parts - 1:
+            for r in range(xn - 1):
+                fo = 2 * ((x + r + 1) % xn) + k
+                for j in range(h * per, (h + 1) * per):
+                    blk = rows(x, k, vd, j)
+                    go(remote(blk, blk, x_send.at[r, j + per], recv.at[r, 3, j], v, fo))
         go(remote(half(x, k, h), half(x, k, h), own_sems.at[0, h], own_sems.at[1, h], v, sib))
     loads[2].start()
 
     def src_of(r):
         return (x + xn - r - 1) % xn
 
-    vd = vy + vz - v
     owners = (v, vy, vz, vd)
 
     def arrive(r, rel, j):
         blk = rows(src_of(r), k, owners[rel], j)
         remote(blk, blk, x_send.at[r, j], recv.at[r, rel, j], v, f).wait_recv()
         first = j % per < per // 2
+        relay = j // per < parts - 1
         if rel == 0:
             go(remote(blk, blk, y_send.at[r, 0, j], recv.at[r, 1, j], vy, f))
             go(remote(blk, blk, z_send.at[r, 0, j], recv.at[r, 2, j], vz, f))
-        if rel == 1 and first:
+        if rel == 1 and relay and first:
             go(remote(blk, blk, z_send.at[r, 1, j], recv.at[r, 3, j], vz, f))
-        if rel == 2 and not first:
+        if rel == 2 and relay and not first:
             go(remote(blk, blk, y_send.at[r, 1, j], recv.at[r, 3, j], vy, f))
         go(remote(blk, blk, s_send.at[r, rel, j], s_recv.at[r, rel, j], v, sib))
 
@@ -235,7 +242,7 @@
             arrivals((1, 2), (2, 2))
         m = tiles(src_of(r), 0, mid, nt, m)
         finish(src_of(r), 0, m)
-    arrivals((1, 3), (2, 3), (3, 2), (3, 3))
+    arrivals((3, 2), (3, 3), (1, 3), (2, 3))
     for r in every:
         passed(r, 1)
         finish(src_of(r), 1, tiles(src_of(r), 1, 0, nt, low))
@@ -299,7 +306,8 @@
     loads[2].wait()
 
     def score(p, c):
-        g = (f + p) % nf
+        t = p + 1
+        g = 2 * ((x + t // 2) % xn) + (k + 1 + t % 2) % 2
         part[g] = lax.dot_general(
             qgm[...], gs[pl.ds(pl.multiple_of(g * eo, eo), eo), :], NT, preferred_element_type=F32)
 
@@ -376,7 +384,7 @@
                 pltpu.VMEM((nf, SEQS, eo), F32),
                 pltpu.VMEM((nf, SEQS, eo), F32),
                 dma((3 + parts,)),
-                dma((xn - 1, SUBS)),
+                dma((xn - 1, SUBS + SUBS // parts)),
                 dma((xn - 1, 2, SUBS)),
                 dma((xn - 1, 2, SUBS)),
                 dma((xn - 1, 4, SUBS)),

time: 65.1 us -> 62.2 us (0.955)
  Pallas kernels: 63 us -> 60.6 us
    pallas_call x1, Pallas kernels: 63 us -> 60.6 us  [on_device(): pl.pallas_call(functools.partial(kernel, nv, nf), out_shape=jax.ShapeDtyp...]
where the time goes in v4:
time: 62.2 us; the launch traced here: 62 us
  Pallas kernels  60.6 us (97%)
  local copies, waits for them, and re-layouts  1.38 us (2%)
    pallas_call x1, Pallas kernels, on_device(): pl.pallas_call(functools.partial(kernel, nv, nf), out_shape=jax.ShapeDtyp...  60.6 us
    unnamed x1, local copies, waits for them, and re-layouts  1.38 us

profile of v4, /device:TPU:0, one launch (start us, length us, event | category | flops | bytes accessed | tf_op | source)
XLA Modules:
  0.0 62.0 jit_solution(15221097613084357324)
XLA Ops:
  0.0 60.6 %shard_map.73 = f32[16,512]{1,0:T(8,128)} custom-call(bf16[256,4096]{1,0:T(8,128)(2,1)} %hid_in.1, bf16[1024,4096]{1,0:T(8,128)(2,1)} %head_in.1, bf16[1024,128]{1,0:T(8,128)(2,1)} %oproj.1, bf16[4096,128]{1,0:T(8,128)(2,1)} %iproj_in.1, s32[8,1,128]{2,1,0:T(1,128)} %bitcast.4, s32[8,1,128]{2,1,0:T(1,128)} %bitcast.5, bf16[2048,4096]{1,0:T(8,128)(2,1)} %gs_in.1), custom_call_target="tpu_custom_call" | custom-call | tf_op jit(solution)/shard_map/pallas_call | solution.py:359
  60.6 1.4 %copy.9 = f32[512,16]{0,1:T(8,128)} copy(f32[512,16]{0,1:T(8,128)} %bitcast.3) | data formatting | bytes 65536
